TPU v7x, 256 devices: a whole 4x4x8 slice. The times are simulated.
256 devices in a mesh: ifg: 8 (over x, core), rows: 32 (over y, z).
Axes of the slice: x: 4, y: 4, z: 8, core: 2. Of those that a mesh axis runs over, the one named last changes fastest.
Arguments:
- phase: bfloat16 [512, 256, 1024], P('ifg', 'rows')
- coherence: bfloat16 [512, 256, 1024], P('ifg', 'rows'), may hold values from 0.0996 to 0.95
- height: float32 [256, 1024], P('rows')
- gap_mask: int32 [512, 256], P('ifg', 'rows'), may hold values 0 or 1
- date_pairs: int32 [512, 2], replicated, may hold values from 0 to 299, as said below
Outputs:
- displacement: float32 [300, 256, 1024], P(None, 'rows', 'ifg')
- topo_slope: float32 [512], P('ifg')
Inputs may be any that keep to these rules, and one draw needn't show every extreme that they name: date_pairs[i, 0] < date_pairs[i, 1] for every interferogram.
All inputs are finite; a program needn't handle non-finite values. No bound on the sum of `gap_mask` on one device may be relied on, other than what follows from the above.
Results may differ from a plain program's by a relative error of at most 0.0028.
Values may be sent and summed in bfloat16 or wider, within the bound.
No kernel may reach another device: no remote copies, remote signals or barrier semaphores. Data moves between devices by JAX's collectives and lax.ppermute only.
A program may use at most 128 MiB of HBM per device.

v0:
```python
import jax
import jax.numpy as jnp
from jax import lax
from jax.sharding import PartitionSpec as P

DATES = 300
ITERS = 3
SMOOTHING_WEIGHT = 0.5
RIDGE_WEIGHT = 0.05
precise = lax.Precision.HIGHEST


def extended(block, sides, width):
    for axis, dim in sides:
        count = lax.axis_size(axis)
        forward = [(i, i + 1) for i in range(count - 1)]
        backward = [(target, source) for source, target in forward]
        low = lax.ppermute(
            lax.slice_in_dim(block, block.shape[dim] - width, None, axis=dim), axis, forward
        )
        high = lax.ppermute(lax.slice_in_dim(block, 0, width, axis=dim), axis, backward)
        block = jnp.concatenate([low, block, high], axis=dim)
    return block


def box_sum(padded):
    row_sum = padded[..., :-2, :] + padded[..., 1:-1, :] + padded[..., 2:, :]
    return row_sum[..., :-2] + row_sum[..., 1:-1] + row_sum[..., 2:]


def smooth_parts(padded):
    phase_pad = padded[0].astype(jnp.float32)
    coher_pad = padded[1].astype(jnp.float32)
    top_sum = box_sum(coher_pad * phase_pad)
    low_sum = box_sum(coher_pad)
    return (top_sum / low_sum, low_sum / 9.0)


def moments(smooth, mean_coh, terrain):
    top_sum = jnp.sum(mean_coh * smooth * terrain[None], axis=(1, 2))
    low_sum = jnp.sum(mean_coh * terrain[None] * terrain[None], axis=(1, 2))
    return (top_sum, low_sum)


def correct(smooth, mean_coh, topo_slope, terrain, mask_rows):
    corrected = (smooth - topo_slope[:, None, None] * terrain[None]).astype(jnp.bfloat16)
    weights = (mask_rows.astype(jnp.float32)[:, :, None] * mean_coh).astype(jnp.bfloat16)
    return (corrected, weights)


def residual_norm(current):
    return lax.psum(jnp.sum(current * current), ("ifg", "rows"))


def per_device(phase, coherence, height, gap_mask, date_pairs):
    stacked = jnp.stack([phase, coherence])
    padded = extended(stacked, (("rows", 2),), 1)
    padded = jnp.pad(padded, ((0, 0), (0, 0), (0, 0), (1, 1)))
    smooth, mean_coh = smooth_parts(padded)
    top_sum, low_sum = moments(smooth, mean_coh, height)
    top_sum, low_sum = lax.psum((top_sum, low_sum), "rows")
    topo_slope = top_sum / low_sum
    corrected, weights = correct(smooth, mean_coh, topo_slope, height, gap_mask)
    corrected, weights = (
        lax.all_to_all(corrected, "ifg", split_axis=2, concat_axis=0, tiled=True),
        lax.all_to_all(weights, "ifg", split_axis=2, concat_axis=0, tiled=True),
    )
    ifg_count, row_count, col_count = weights.shape
    pixels = row_count * col_count
    dates_axis = jnp.arange(DATES, dtype=jnp.int32)
    design = (dates_axis[None, :] == date_pairs[:, 1:2]).astype(jnp.float32) - (
        dates_axis[None, :] == date_pairs[:, 0:1]
    ).astype(jnp.float32)
    weight_flat = weights.reshape(ifg_count, pixels)

    def back_project(values):
        return lax.dot_general(
            design,
            values,
            (((0,), (0,)), ((), ())),
            precision=precise,
            preferred_element_type=jnp.float32,
        )

    right_side = back_project(
        weight_flat.astype(jnp.float32) * corrected.reshape(ifg_count, pixels).astype(jnp.float32)
    )
    displacement = jnp.zeros_like(right_side)
    residual = right_side
    direction = right_side
    norm_now = residual_norm(residual)
    for sweep_index in range(ITERS):
        cube_grid = direction.reshape(DATES, row_count, col_count)
        padded_cube = extended(cube_grid, (("ifg", 2), ("rows", 1)), 1)
        neighbours = (
            padded_cube[:, 2:, 1:-1]
            + padded_cube[:, :-2, 1:-1]
            + padded_cube[:, 1:-1, 2:]
            + padded_cube[:, 1:-1, :-2]
        )
        spread = (4.0 * cube_grid - neighbours).reshape(DATES, pixels)
        differences = jnp.dot(
            design, direction, precision=precise, preferred_element_type=jnp.float32
        )
        mapped = back_project(differences * weight_flat)
        mapped = mapped + SMOOTHING_WEIGHT * spread + RIDGE_WEIGHT * direction
        step_size = norm_now / lax.psum(jnp.sum(direction * mapped), ("ifg", "rows"))
        displacement = displacement + step_size * direction
        residual = residual - step_size * mapped
        norm_next = residual_norm(residual)
        direction = residual + norm_next / norm_now * direction
        norm_now = norm_next
    return (displacement.reshape(DATES, row_count, col_count), topo_slope)


def solution(mesh):
    placed = (
        P("ifg", "rows", None),
        P("ifg", "rows", None),
        P("rows", None),
        P("ifg", "rows"),
        P(),
    )
    return jax.shard_map(
        per_device,
        mesh=mesh,
        in_specs=placed,
        out_specs=(P(None, "rows", "ifg"), P("ifg")),
        check_vma=False,
    )
```

profile of v0, /device:TPU:1, one launch (start us, length us, event | category | flops | bytes accessed | tf_op | source)
XLA Modules:
  0.0 687.9 jit_solution(10291353964235521718)
XLA Ops:
  0.6 3.4 fusion.36
  7.0 5.7 collective-permute-start
  13.4 5.1 copy.95
  23.0 11.1 %fusion.5 = bf16[2,64,10,1026]{1,2,3,0:T(8,128)(2,1)S(1)} fusion(bf16[2,64,1,1024]{1,2,3,0:T(2,128)(2,1)S(1)} %copy.96, bf16[2,64,8,1024]{1,2,3,0:T(8,128)(2,1)} %copy.95, bf16[2,64,1,1024]{1,2,3,0:T(2,128)(2,1)S(1)} %copy.94), kind=kLoop, calls=%fused_computation.7 | loop fusion | flops 15759360 | bytes 5248000 | tf_op jit(solution)/shard_map/concatenate | solution.py:22
  44.3 6.9 %all-to-all-start = ((bf16[8,2,32768]{2,1,0:T(2,128)(2,1)}), bf16[8,2,32768]{2,1,0:T(2,128)(2,1)}, u32[]{:S(2)}, u32[]{:S(2)}) async-start(bf16[8,2,32768]{2,1,0:T(2,128)(2,1)} %reshape.56), calls=%async_computation | async-start | bytes 2097152 | tf_op jit(solution)/shard_map/all_to_all | solution.py:66
  51.2 10.1 %multiply_reduce_fusion = (f32[64]{0:T(128)S(1)}, f32[64]{0:T(128)S(1)}, f32[64,8,1024]{0,1,2:T(8,128)}) fusion(f32[64,8,1024]{0,1,2:T(8,128)} %get-tuple-element.13, f32[8,1024]{0,1:T(8,128)S(1)} %copy.99, f32[8,1024]{0,1:T(8,128)S(1)} %copy.98, f32[64,8,1026]{0,1,2:T(8,128)} %slice_add_fusion), kind=kLoop, calls=%fused_computation.22 | loop fusion | flops 5242752 | bytes 10551808 | tf_op jit(solution)/shard_map/reduce_sum | solution.py:41
  61.3 63.6 %all-reduce.2 = (f32[64]{0:T(128)S(1)}, f32[64]{0:T(128)S(1)}) all-reduce(f32[64]{0:T(128)S(1)} %get-tuple-element.3, f32[64]{0:T(128)S(1)} %get-tuple-element.2), channel_id=1, replica_groups=mesh['ifg'=8,'rows'=32] {'rows'}, use_global_device_ids=true, to_apply=%region_1.2 | all-reduce | flops 128 | bytes 1024 | tf_op jit(solution)/shard_map/psum | solution.py:61
  130.4 19.1 %all-to-all-start.1 = ((bf16[8,2,32768]{2,1,0:T(2,128)(2,1)}), bf16[8,2,32768]{2,1,0:T(2,128)(2,1)S(1)}, u32[]{:S(2)}, u32[]{:S(2)}) async-start(bf16[8,2,32768]{2,1,0:T(2,128)(2,1)} %reshape.54), calls=%async_computation.1 | async-start | bytes 2097152 | tf_op jit(solution)/shard_map/all_to_all | solution.py:65
  149.6 4.3 reshape.57
  156.5 8.1 %all-to-all-done.1 = bf16[8,2,32768]{2,1,0:T(2,128)(2,1)S(1)} async-done(((bf16[8,2,32768]{2,1,0:T(2,128)(2,1)}), bf16[8,2,32768]{2,1,0:T(2,128)(2,1)S(1)}, u32[]{:S(2)}, u32[]{:S(2)}) %all-to-all-start.1) | async-done | bytes 1048608 | tf_op jit(solution)/shard_map/all_to_all | solution.py:65
  167.3 3.5 copy.100
  170.7 4.5 fusion.8
  179.1 3.0 collective-permute-start.2
  188.2 2.9 copy.101
  193.5 4.3 collective-permute-start.5
  197.9 4.9 fusion.35
  207.5 6.4 multiply_reduce_fusion.6
  213.8 73.8 %all-reduce.1 = (f32[]{:T(128)}, f32[]{:T(128)}) all-reduce(f32[]{:T(128)} %get-tuple-element.5, f32[]{:T(128)} %get-tuple-element.4), channel_id=1, replica_groups=mesh['ifg'=8,'rows'=32] {'ifg','rows'}, use_global_device_ids=true, to_apply=%region_5.6 | all-reduce | flops 2 | bytes 16 | tf_op jit(solution)/shard_map/psum | solution.py:52
  288.9 3.7 multiply_reduce_fusion.5
  292.7 73.1 %psum.60 = f32[]{:T(128)} all-reduce(f32[]{:T(128)} %get-tuple-element.10), channel_id=1, replica_groups=mesh['ifg'=8,'rows'=32] {'ifg','rows'}, use_global_device_ids=true, to_apply=%region_9.10 | all-reduce | flops 1 | bytes 8 | tf_op jit(solution)/shard_map/psum | solution.py:52
  386.6 4.5 collective-permute-start.9
  391.1 4.9 fusion.34
  400.7 6.9 multiply_reduce_fusion.4
  407.6 76.5 %psum.61 = f32[]{:T(128)} all-reduce(f32[]{:T(128)} %get-tuple-element.32), channel_id=1, replica_groups=mesh['ifg'=8,'rows'=32] {'ifg','rows'}, use_global_device_ids=true, to_apply=%region_11.12 | all-reduce | flops 1 | bytes 8 | tf_op jit(solution)/shard_map/psum | solution.py:107
  485.3 3.1 multiply_reduce_fusion.3
  488.3 73.3 %psum.62 = f32[]{:T(128)} all-reduce(f32[]{:T(128)} %multiply_reduce_fusion.3), channel_id=1, replica_groups=mesh['ifg'=8,'rows'=32] {'ifg','rows'}, use_global_device_ids=true, to_apply=%region_13.14 | all-reduce | flops 1 | bytes 8 | tf_op jit(solution)/shard_map/psum | solution.py:52
  571.3 3.5 collective-permute-start.10
  576.9 6.2 fusion.33
  589.6 4.1 collective-permute-start.13
  593.7 5.9 fusion.13
  604.3 3.0 multiply_reduce_fusion.2
  607.3 76.0 %psum.63 = f32[]{:T(128)} all-reduce(f32[]{:T(128)} %multiply_reduce_fusion.2), channel_id=1, replica_groups=mesh['ifg'=8,'rows'=32] {'ifg','rows'}, use_global_device_ids=true, to_apply=%region_15.16 | all-reduce | flops 1 | bytes 8 | tf_op jit(solution)/shard_map/psum | solution.py:107
  (111 shorter events, 94.8 us)
Async XLA Ops:
  0.6 12.1 %copy-start.10 = (bf16[64,8,1024]{2,1,0:T(8,128)(2,1)S(1)}, bf16[64,8,1024]{2,1,0:T(8,128)(2,1)}, u32[]{:S(2)}) copy-start(bf16[64,8,1024]{2,1,0:T(8,128)(2,1)} %param.6) | copy-start | bytes 3145732
  4.1 8.6 %copy-start.11 = (f32[8,1024]{1,0:T(8,128)S(1)}, f32[8,1024]{1,0:T(8,128)}, u32[]{:S(2)}) copy-start(f32[8,1024]{1,0:T(8,128)} %param.7) | copy-start | bytes 98308
  4.1 8.6 %copy-start.9 = (bf16[64,8,1024]{2,1,0:T(8,128)(2,1)S(1)}, bf16[64,8,1024]{2,1,0:T(8,128)(2,1)}, u32[]{:S(2)}) copy-start(bf16[64,8,1024]{2,1,0:T(8,128)(2,1)} %param.5) | copy-start | bytes 3145732
  4.9 15.8 %collective-permute-start.1 = (bf16[2,64,1,1024]{3,1,2,0:T(8,128)(2,1)}, bf16[2,64,1,1024]{3,1,2,0:T(8,128)(2,1)}, u32[]{:S(2)}, u32[]{:S(2)}) collective-permute-start(bf16[2,64,1,1024]{3,1,2,0:T(8,128)(2,1)} %copy.138), channel_id=1, source_target_pairs={{1,0},{2,1},{3,2},{4,3},{5,4},{6,5},{7,6},{8,7},{9,8},{10,9},{11,1... | collective-permute-start | bytes 786440 | tf_op jit(solution)/shard_map/ppermute | solution.py:21
  7.0 11.5 %collective-permute-start = (bf16[2,64,1,1024]{3,1,2,0:T(8,128)(2,1)}, bf16[2,64,1,1024]{3,1,2,0:T(8,128)(2,1)}, u32[]{:S(2)}, u32[]{:S(2)}) collective-permute-start(bf16[2,64,1,1024]{3,1,2,0:T(8,128)(2,1)} %copy.137), channel_id=1, source_target_pairs={{0,1},{1,2},{2,3},{3,4},{4,5},{5,6},{6,7},{7,8},{8,9},{9,10},{10,1... | collective-permute-start | bytes 786440 | tf_op jit(solution)/shard_map/ppermute | solution.py:18
  13.4 5.2 copy-start.12
  44.3 86.1 %all-to-all-start = ((bf16[8,2,32768]{2,1,0:T(2,128)(2,1)}), bf16[8,2,32768]{2,1,0:T(2,128)(2,1)}, u32[]{:S(2)}, u32[]{:S(2)}) async-start(bf16[8,2,32768]{2,1,0:T(2,128)(2,1)} %reshape.56), calls=%async_computation | async-start | bytes 2097152 | tf_op jit(solution)/shard_map/all_to_all | solution.py:66
  124.9 2.9 copy-start.14
  130.4 19.1 %copy-start.13 = (s32[512,2]{0,1:T(2,128)S(1)}, s32[512,2]{0,1:T(2,128)}, u32[]{:S(2)}) copy-start(s32[512,2]{0,1:T(2,128)} %param.9) | copy-start | bytes 12292
  130.4 34.2 %all-to-all-start.1 = ((bf16[8,2,32768]{2,1,0:T(2,128)(2,1)}), bf16[8,2,32768]{2,1,0:T(2,128)(2,1)S(1)}, u32[]{:S(2)}, u32[]{:S(2)}) async-start(bf16[8,2,32768]{2,1,0:T(2,128)(2,1)} %reshape.54), calls=%async_computation.1 | async-start | bytes 2097152 | tf_op jit(solution)/shard_map/all_to_all | solution.py:65
  156.5 51.0 %copy-start = (f32[64,8,8,128]{3,1,0,2:T(8,128)}, f32[64,8,8,128]{3,1,0,2:T(8,128)S(1)}, u32[]{:S(2)}) copy-start(f32[64,8,8,128]{3,1,0,2:T(8,128)S(1)} %copy.97) | copy-start | bytes 6291460
  175.5 1.9 copy-start.4
  179.1 12.0 %collective-permute-start.2 = (f32[300,8,1]{0,1,2:T(8,128)S(1)}, f32[300,8,1]{0,1,2:T(8,128)S(1)}, u32[]{:S(2)}, u32[]{:S(2)}) collective-permute-start(f32[300,8,1]{0,1,2:T(8,128)S(1)} %copy.139), channel_id=1, source_target_pairs={{0,32},{32,64},{64,96},{96,128},{128,160},{160,192},{192,224},{1,3... | collective-permute-start | bytes 28808 | tf_op jit(solution)/shard_map/ppermute | solution.py:18
  183.8 7.3 %collective-permute-start.3 = (f32[300,8,1]{0,1,2:T(8,128)S(1)}, f32[300,8,1]{0,1,2:T(8,128)S(1)}, u32[]{:S(2)}, u32[]{:S(2)}) collective-permute-start(f32[300,8,1]{0,1,2:T(8,128)S(1)} %copy.140), channel_id=1, source_target_pairs={{32,0},{64,32},{96,64},{128,96},{160,128},{192,160},{224,192},{33,... | collective-permute-start | bytes 28808 | tf_op jit(solution)/shard_map/ppermute | solution.py:21
  192.2 10.5 %collective-permute-start.4 = (f32[300,1,130]{0,2,1:T(8,128)S(1)}, f32[300,1,130]{0,2,1:T(8,128)S(1)}, u32[]{:S(2)}, u32[]{:S(2)}) collective-permute-start(f32[300,1,130]{0,2,1:T(8,128)S(1)} %get-tuple-element.21), channel_id=1, source_target_pairs={{1,0},{2,1},{3,2},{4,3},{5,4},{6,5},{7,6},{8,7},{9,8},{10,9},{11,1... | collective-permute-start | bytes 468008 | tf_op jit(solution)/shard_map/ppermute | solution.py:21
  193.5 9.2 %copy-start.7 = (f32[300,8,128]{0,2,1:T(8,128)S(1)}, f32[300,8,128]{0,2,1:T(8,128)}, u32[]{:S(2)}) copy-start(f32[300,8,128]{0,2,1:T(8,128)} %copy.101) | copy-start | bytes 3686404
  193.5 9.2 %collective-permute-start.5 = (f32[300,1,130]{0,2,1:T(8,128)S(1)}, f32[300,1,130]{0,2,1:T(8,128)S(1)}, u32[]{:S(2)}, u32[]{:S(2)}) collective-permute-start(f32[300,1,130]{0,2,1:T(8,128)S(1)} %get-tuple-element.22), channel_id=1, source_target_pairs={{0,1},{1,2},{2,3},{3,4},{4,5},{5,6},{6,7},{7,8},{8,9},{9,10},{10,1... | collective-permute-start | bytes 468008 | tf_op jit(solution)/shard_map/ppermute | solution.py:18
  368.8 1.9 copy-start.5
  372.4 11.7 %collective-permute-start.6 = (f32[300,8,1]{0,1,2:T(8,128)S(1)}, f32[300,8,1]{0,1,2:T(8,128)S(1)}, u32[]{:S(2)}, u32[]{:S(2)}) collective-permute-start(f32[300,8,1]{0,1,2:T(8,128)S(1)} %copy.141), channel_id=1, source_target_pairs={{0,32},{32,64},{64,96},{96,128},{128,160},{160,192},{192,224},{1,3... | collective-permute-start | bytes 28808 | tf_op jit(solution)/shard_map/ppermute | solution.py:18
  376.9 7.3 %collective-permute-start.7 = (f32[300,8,1]{0,1,2:T(8,128)S(1)}, f32[300,8,1]{0,1,2:T(8,128)S(1)}, u32[]{:S(2)}, u32[]{:S(2)}) collective-permute-start(f32[300,8,1]{0,1,2:T(8,128)S(1)} %copy.142), channel_id=1, source_target_pairs={{32,0},{64,32},{96,64},{128,96},{160,128},{192,160},{224,192},{33,... | collective-permute-start | bytes 28808 | tf_op jit(solution)/shard_map/ppermute | solution.py:21
  385.3 10.7 %collective-permute-start.8 = (f32[300,1,130]{0,2,1:T(8,128)S(1)}, f32[300,1,130]{0,2,1:T(8,128)S(1)}, u32[]{:S(2)}, u32[]{:S(2)}) collective-permute-start(f32[300,1,130]{0,2,1:T(8,128)S(1)} %get-tuple-element.19), channel_id=1, source_target_pairs={{1,0},{2,1},{3,2},{4,3},{5,4},{6,5},{7,6},{8,7},{9,8},{10,9},{11,1... | collective-permute-start | bytes 468008 | tf_op jit(solution)/shard_map/ppermute | solution.py:21
  386.6 9.4 %copy-start.8 = (f32[300,8,128]{0,2,1:T(8,128)S(1)}, f32[300,8,128]{0,2,1:T(8,128)}, u32[]{:S(2)}) copy-start(f32[300,8,128]{0,2,1:T(8,128)} %copy.112) | copy-start | bytes 3686404
  386.6 9.4 %collective-permute-start.9 = (f32[300,1,130]{0,2,1:T(8,128)S(1)}, f32[300,1,130]{0,2,1:T(8,128)S(1)}, u32[]{:S(2)}, u32[]{:S(2)}) collective-permute-start(f32[300,1,130]{0,2,1:T(8,128)S(1)} %get-tuple-element.20), channel_id=1, source_target_pairs={{0,1},{1,2},{2,3},{3,4},{4,5},{5,6},{6,7},{7,8},{8,9},{9,10},{10,1... | collective-permute-start | bytes 468008 | tf_op jit(solution)/shard_map/ppermute | solution.py:18
  565.5 2.3 copy-start.1
  565.7 2.0 copy-start.2
  571.3 11.8 %copy-start.3 = (f32[38,8,8,128]{3,2,1,0:T(8,128)S(1)}, f32[38,8,8,128]{3,2,1,0:T(8,128)}, u32[]{:S(2)}) copy-start(f32[38,8,8,128]{3,2,1,0:T(8,128)} %copy-done.2) | copy-start | bytes 3735556
  571.3 15.9 %collective-permute-start.10 = (f32[300,8,1]{0,1,2:T(8,128)S(1)}, f32[300,8,1]{0,1,2:T(8,128)S(1)}, u32[]{:S(2)}, u32[]{:S(2)}) collective-permute-start(f32[300,8,1]{0,1,2:T(8,128)S(1)} %copy.143), channel_id=1, source_target_pairs={{0,32},{32,64},{64,96},{96,128},{128,160},{160,192},{192,224},{1,3... | collective-permute-start | bytes 28808 | tf_op jit(solution)/shard_map/ppermute | solution.py:18
  574.8 12.3 %collective-permute-start.11 = (f32[300,8,1]{0,1,2:T(8,128)S(1)}, f32[300,8,1]{0,1,2:T(8,128)S(1)}, u32[]{:S(2)}, u32[]{:S(2)}) collective-permute-start(f32[300,8,1]{0,1,2:T(8,128)S(1)} %copy.144), channel_id=1, source_target_pairs={{32,0},{64,32},{96,64},{128,96},{160,128},{192,160},{224,192},{33,... | collective-permute-start | bytes 28808 | tf_op jit(solution)/shard_map/ppermute | solution.py:21
  588.3 11.3 %collective-permute-start.12 = (f32[300,1,130]{0,2,1:T(8,128)S(1)}, f32[300,1,130]{0,2,1:T(8,128)S(1)}, u32[]{:S(2)}, u32[]{:S(2)}) collective-permute-start(f32[300,1,130]{0,2,1:T(8,128)S(1)} %get-tuple-element.17), channel_id=1, source_target_pairs={{1,0},{2,1},{3,2},{4,3},{5,4},{6,5},{7,6},{8,7},{9,8},{10,9},{11,1... | collective-permute-start | bytes 468008 | tf_op jit(solution)/shard_map/ppermute | solution.py:21
  589.6 10.0 %copy-start.6 = (f32[300,8,128]{0,2,1:T(8,128)S(1)}, f32[300,8,128]{0,2,1:T(8,128)}, u32[]{:S(2)}) copy-start(f32[300,8,128]{0,2,1:T(8,128)} %copy.123) | copy-start | bytes 3686404
  589.6 10.0 %collective-permute-start.13 = (f32[300,1,130]{0,2,1:T(8,128)S(1)}, f32[300,1,130]{0,2,1:T(8,128)S(1)}, u32[]{:S(2)}, u32[]{:S(2)}) collective-permute-start(f32[300,1,130]{0,2,1:T(8,128)S(1)} %get-tuple-element.18), channel_id=1, source_target_pairs={{0,1},{1,2},{2,3},{3,4},{4,5},{5,6},{6,7},{7,8},{8,9},{9,10},{10,1... | collective-permute-start | bytes 468008 | tf_op jit(solution)/shard_map/ppermute | solution.py:18
where the time goes:
time: 697 us; the launch traced here: 688 us
  blocking collectives  436 us (63%)
  local copies, waits for them, and re-layouts  71.9 us (10%)
  starting transfers between devices  65 us (9%)
  other arithmetic  59.4 us (9%)
  matrix products  39.5 us (6%)
  waiting for transfers between devices  8.14 us (1%)
  between operations  7.69 us (1%)
    psum x3, blocking collectives, residual_norm(): return lax.psum(jnp.sum(current * current), ('ifg', 'rows'))  220 us
    psum x2, blocking collectives, per_device(): lax.psum(jnp.sum(direction * mapped), ('ifg', 'rows'))  152 us
    psum x1, blocking collectives, per_device(): top_sum, low_sum = lax.psum((top_sum, low_sum), 'rows')  63.6 us
    ppermute x7, starting transfers between devices, extended(): lax.ppermute(lax.slice_in_dim(block, block.shape[dim] - width, None, axis...  27.9 us
    unnamed x47, local copies, waits for them, and re-layouts  25.7 us
    dot_general x4, matrix products, back_project(): lax.dot_general(design, values, (((0,), (0,)), ((), ())), precision=preci...  23.6 us
    all_to_all x1, starting transfers between devices, per_device(): lax.all_to_all(corrected, 'ifg', split_axis=2, concat_axis=0, tiled=True)  19.1 us
    dot_general x3, matrix products, per_device(): jnp.dot(design, direction, precision=precise, preferred_element_type=jnp....  15.9 us
  transfers between devices with their start and end apart: 16, of which 1 were waited for; matrix products, arithmetic and copies ran while one was open for 10% of the time, Pallas kernels for 0%

commit v1 on v0

--- a/solution.py
+++ b/solution.py
@@ -62,7 +62,12 @@
     topo_slope = top_sum / low_sum
     corrected, weights = correct(smooth, mean_coh, topo_slope, height, gap_mask)
     corrected, weights = (
-        lax.all_to_all(corrected, "ifg", split_axis=2, concat_axis=0, tiled=True),
+        jnp.concatenate(
+            lax.all_to_all(
+                jnp.stack(jnp.split(corrected, lax.axis_size("ifg"), axis=2)), "ifg", 0, 0
+            ),
+            axis=0,
+        ),
         lax.all_to_all(weights, "ifg", split_axis=2, concat_axis=0, tiled=True),
     )
     ifg_count, row_count, col_count = weights.shape

time: 697 us -> 715 us (1.026)
  waiting for transfers between devices: 8.14 us -> 26 us
  other arithmetic: 59.4 us -> 52.2 us
    all_to_all x1, waiting for transfers between devices: 0.01 us -> 13.5 us  [per_device(): lax.all_to_all(weights, 'ifg', split_axis=2, concat_axis=0, tiled=True)]
    another operation x0 -> x10, local copies, waits for them, and re-layouts: none -> 9.8 us  [per_device(): jnp.stack(jnp.split(corrected, lax.axis_size('ifg'), axis=2))]
    unnamed x47 -> x56, local copies, waits for them, and re-layouts: 25.7 us -> 25.2 us
  transfers between devices with their start and end apart: 16 -> 16, of which waited for: 1 -> 2; matrix products, arithmetic and copies ran while one was open for 10% -> 8% of each run, Pallas kernels for 0% -> 0%
where the time goes in v1:
time: 715 us; the launch traced here: 704 us
  blocking collectives  437 us (61%)
  local copies, waits for them, and re-layouts  77.7 us (11%)
  starting transfers between devices  63.4 us (9%)
  other arithmetic  52.2 us (7%)
  matrix products  40.2 us (6%)
  waiting for transfers between devices  26 us (4%)
  between operations  7.79 us (1%)
    psum x3, blocking collectives, residual_norm(): return lax.psum(jnp.sum(current * current), ('ifg', 'rows'))  220 us
    psum x2, blocking collectives, per_device(): lax.psum(jnp.sum(direction * mapped), ('ifg', 'rows'))  152 us
    psum x1, blocking collectives, per_device(): top_sum, low_sum = lax.psum((top_sum, low_sum), 'rows')  64.3 us
    ppermute x7, starting transfers between devices, extended(): lax.ppermute(lax.slice_in_dim(block, block.shape[dim] - width, None, axis...  27.7 us
    unnamed x56, local copies, waits for them, and re-layouts  25.2 us
    dot_general x4, matrix products, back_project(): lax.dot_general(design, values, (((0,), (0,)), ((), ())), precision=preci...  24.3 us
    all_to_all x1, starting transfers between devices, per_device(): lax.all_to_all(jnp.stack(jnp.split(corrected, lax.axis_size('ifg'), axis=...  20.2 us
    dot_general x3, matrix products, per_device(): jnp.dot(design, direction, precision=precise, preferred_element_type=jnp....  15.9 us
  transfers between devices with their start and end apart: 16, of which 2 were waited for; matrix products, arithmetic and copies ran while one was open for 8% of the time, Pallas kernels for 0%

profile of v1, /device:TPU:1, one launch (start us, length us, event | category | flops | bytes accessed | tf_op | source)
XLA Modules:
  0.0 704.4 jit_solution(8171989574921765945)
XLA Ops:
  0.6 3.3 fusion.36
  6.9 5.7 collective-permute-start
  13.2 5.1 copy.138
  22.9 11.1 %fusion.5 = bf16[2,64,10,1026]{1,2,3,0:T(8,128)(2,1)S(1)} fusion(bf16[2,64,1,1024]{1,2,3,0:T(2,128)(2,1)S(1)} %copy.139, bf16[2,64,8,1024]{1,2,3,0:T(8,128)(2,1)} %copy.138, bf16[2,64,1,1024]{1,2,3,0:T(2,128)(2,1)S(1)} %copy.137), kind=kLoop, calls=%fused_computation.7 | loop fusion | flops 15759360 | bytes 5248000 | tf_op jit(solution)/shard_map/concatenate | solution.py:22
  38.1 4.9 multiply_reduce_fusion
  43.0 64.3 %all-reduce.2 = (f32[64]{0:T(128)S(1)}, f32[64]{0:T(128)S(1)}) all-reduce(f32[64]{0:T(128)S(1)} %get-tuple-element.3, f32[64]{0:T(128)S(1)} %get-tuple-element.2), channel_id=1, replica_groups=mesh['ifg'=8,'rows'=32] {'rows'}, use_global_device_ids=true, to_apply=%region_1.2 | all-reduce | flops 128 | bytes 1024 | tf_op jit(solution)/shard_map/psum | solution.py:61
  126.5 20.2 %all-to-all-start.1 = ((bf16[8,64,8,128]{3,2,1,0:T(8,128)(2,1)}), bf16[8,64,8,128]{3,2,1,0:T(8,128)(2,1)S(1)}, u32[]{:S(2)}, u32[]{:S(2)}) async-start(bf16[8,64,8,128]{3,2,1,0:T(8,128)(2,1)} %constant_dynamic-update-slice_fusion), calls=%async_computation.1 | async-start | bytes 2097152 | tf_op jit(solution)/shard_map/all_to_all | solution.py:66
  149.3 12.5 %all-to-all-done.1 = bf16[8,64,8,128]{3,2,1,0:T(8,128)(2,1)S(1)} async-done(((bf16[8,64,8,128]{3,2,1,0:T(8,128)(2,1)}), bf16[8,64,8,128]{3,2,1,0:T(8,128)(2,1)S(1)}, u32[]{:S(2)}, u32[]{:S(2)}) %all-to-all-start.1) | async-done | bytes 1048608 | tf_op jit(solution)/shard_map/all_to_all | solution.py:66
  161.8 4.5 all-to-all-start
  167.9 13.5 %all-to-all-done = bf16[8,2,32768]{2,1,0:T(2,128)(2,1)S(1)} async-done(((bf16[8,2,32768]{2,1,0:T(2,128)(2,1)}), bf16[8,2,32768]{2,1,0:T(2,128)(2,1)S(1)}, u32[]{:S(2)}, u32[]{:S(2)}) %all-to-all-start) | async-done | bytes 1048608 | tf_op jit(solution)/shard_map/all_to_all | solution.py:71
  186.7 5.3 fusion.8
  195.8 3.0 collective-permute-start.2
  204.9 2.9 copy.151
  210.2 4.1 collective-permute-start.5
  214.4 4.9 fusion.35
  224.0 6.3 multiply_reduce_fusion.6
  230.3 73.9 %all-reduce.1 = (f32[]{:T(128)}, f32[]{:T(128)}) all-reduce(f32[]{:T(128)} %get-tuple-element.5, f32[]{:T(128)} %get-tuple-element.4), channel_id=1, replica_groups=mesh['ifg'=8,'rows'=32] {'ifg','rows'}, use_global_device_ids=true, to_apply=%region_5.6 | all-reduce | flops 2 | bytes 16 | tf_op jit(solution)/shard_map/psum | solution.py:52
  305.5 3.7 multiply_reduce_fusion.5
  309.2 73.0 %psum.60 = f32[]{:T(128)} all-reduce(f32[]{:T(128)} %get-tuple-element.10), channel_id=1, replica_groups=mesh['ifg'=8,'rows'=32] {'ifg','rows'}, use_global_device_ids=true, to_apply=%region_9.10 | all-reduce | flops 1 | bytes 8 | tf_op jit(solution)/shard_map/psum | solution.py:52
  397.7 2.9 copy.162
  403.1 4.5 collective-permute-start.9
  407.6 4.9 fusion.34
  417.2 6.9 multiply_reduce_fusion.4
  424.1 76.5 %psum.61 = f32[]{:T(128)} all-reduce(f32[]{:T(128)} %get-tuple-element.40), channel_id=1, replica_groups=mesh['ifg'=8,'rows'=32] {'ifg','rows'}, use_global_device_ids=true, to_apply=%region_11.12 | all-reduce | flops 1 | bytes 8 | tf_op jit(solution)/shard_map/psum | solution.py:112
  501.8 3.1 multiply_reduce_fusion.3
  504.9 73.5 %psum.62 = f32[]{:T(128)} all-reduce(f32[]{:T(128)} %multiply_reduce_fusion.3), channel_id=1, replica_groups=mesh['ifg'=8,'rows'=32] {'ifg','rows'}, use_global_device_ids=true, to_apply=%region_13.14 | all-reduce | flops 1 | bytes 8 | tf_op jit(solution)/shard_map/psum | solution.py:52
  588.0 3.4 collective-permute-start.10
  593.6 6.2 fusion.33
  606.2 4.1 collective-permute-start.13
  610.4 5.9 fusion.13
  620.9 3.0 multiply_reduce_fusion.2
  623.9 76.0 %psum.63 = f32[]{:T(128)} all-reduce(f32[]{:T(128)} %multiply_reduce_fusion.2), channel_id=1, replica_groups=mesh['ifg'=8,'rows'=32] {'ifg','rows'}, use_global_device_ids=true, to_apply=%region_15.16 | all-reduce | flops 1 | bytes 8 | tf_op jit(solution)/shard_map/psum | solution.py:112
  (130 shorter events, 103.5 us)
Async XLA Ops:
  0.6 12.0 %copy-start.10 = (bf16[64,8,1024]{2,1,0:T(8,128)(2,1)S(1)}, bf16[64,8,1024]{2,1,0:T(8,128)(2,1)}, u32[]{:S(2)}) copy-start(bf16[64,8,1024]{2,1,0:T(8,128)(2,1)} %param.6) | copy-start | bytes 3145732
  4.0 8.6 %copy-start.13 = (f32[8,1024]{1,0:T(8,128)S(1)}, f32[8,1024]{1,0:T(8,128)}, u32[]{:S(2)}) copy-start(f32[8,1024]{1,0:T(8,128)} %param.7) | copy-start | bytes 98308
  4.0 8.6 %copy-start.9 = (bf16[64,8,1024]{2,1,0:T(8,128)(2,1)S(1)}, bf16[64,8,1024]{2,1,0:T(8,128)(2,1)}, u32[]{:S(2)}) copy-start(bf16[64,8,1024]{2,1,0:T(8,128)(2,1)} %param.5) | copy-start | bytes 3145732
  4.8 15.8 %collective-permute-start.1 = (bf16[2,64,1,1024]{3,1,2,0:T(8,128)(2,1)}, bf16[2,64,1,1024]{3,1,2,0:T(8,128)(2,1)}, u32[]{:S(2)}, u32[]{:S(2)}) collective-permute-start(bf16[2,64,1,1024]{3,1,2,0:T(8,128)(2,1)} %copy.188), channel_id=1, source_target_pairs={{1,0},{2,1},{3,2},{4,3},{5,4},{6,5},{7,6},{8,7},{9,8},{10,9},{11,1... | collective-permute-start | bytes 786440 | tf_op jit(solution)/shard_map/ppermute | solution.py:21
  6.9 11.5 %collective-permute-start = (bf16[2,64,1,1024]{3,1,2,0:T(8,128)(2,1)}, bf16[2,64,1,1024]{3,1,2,0:T(8,128)(2,1)}, u32[]{:S(2)}, u32[]{:S(2)}) collective-permute-start(bf16[2,64,1,1024]{3,1,2,0:T(8,128)(2,1)} %copy.187), channel_id=1, source_target_pairs={{0,1},{1,2},{2,3},{3,4},{4,5},{5,6},{6,7},{7,8},{8,9},{9,10},{10,1... | collective-permute-start | bytes 786440 | tf_op jit(solution)/shard_map/ppermute | solution.py:18
  13.2 5.2 copy-start.14
  107.3 2.9 copy-start.16
  118.1 4.2 copy-start.12
  118.1 4.9 copy-start.11
  126.5 35.3 %all-to-all-start.1 = ((bf16[8,64,8,128]{3,2,1,0:T(8,128)(2,1)}), bf16[8,64,8,128]{3,2,1,0:T(8,128)(2,1)S(1)}, u32[]{:S(2)}, u32[]{:S(2)}) async-start(bf16[8,64,8,128]{3,2,1,0:T(8,128)(2,1)} %constant_dynamic-update-slice_fusion), calls=%async_computation.1 | async-start | bytes 2097152 | tf_op jit(solution)/shard_map/all_to_all | solution.py:66
  149.3 17.0 %copy-start.15 = (s32[512,2]{0,1:T(2,128)S(1)}, s32[512,2]{0,1:T(2,128)}, u32[]{:S(2)}) copy-start(s32[512,2]{0,1:T(2,128)} %param.9) | copy-start | bytes 12292
  161.8 19.6 %all-to-all-start = ((bf16[8,2,32768]{2,1,0:T(2,128)(2,1)}), bf16[8,2,32768]{2,1,0:T(2,128)(2,1)S(1)}, u32[]{:S(2)}, u32[]{:S(2)}) async-start(bf16[8,2,32768]{2,1,0:T(2,128)(2,1)} %reshape.49), calls=%async_computation | async-start | bytes 2097152 | tf_op jit(solution)/shard_map/all_to_all | solution.py:71
  186.7 37.3 %copy-start = (f32[64,8,8,128]{3,1,0,2:T(8,128)}, f32[64,8,8,128]{3,1,0,2:T(8,128)S(1)}, u32[]{:S(2)}) copy-start(f32[64,8,8,128]{3,1,0,2:T(8,128)S(1)} %copy.140) | copy-start | bytes 6291460
  192.2 1.8 copy-start.4
  195.8 12.0 %collective-permute-start.2 = (f32[300,8,1]{0,1,2:T(8,128)S(1)}, f32[300,8,1]{0,1,2:T(8,128)S(1)}, u32[]{:S(2)}, u32[]{:S(2)}) collective-permute-start(f32[300,8,1]{0,1,2:T(8,128)S(1)} %copy.189), channel_id=1, source_target_pairs={{0,32},{32,64},{64,96},{96,128},{128,160},{160,192},{192,224},{1,3... | collective-permute-start | bytes 28808 | tf_op jit(solution)/shard_map/ppermute | solution.py:18
  200.5 7.3 %collective-permute-start.3 = (f32[300,8,1]{0,1,2:T(8,128)S(1)}, f32[300,8,1]{0,1,2:T(8,128)S(1)}, u32[]{:S(2)}, u32[]{:S(2)}) collective-permute-start(f32[300,8,1]{0,1,2:T(8,128)S(1)} %copy.190), channel_id=1, source_target_pairs={{32,0},{64,32},{96,64},{128,96},{160,128},{192,160},{224,192},{33,... | collective-permute-start | bytes 28808 | tf_op jit(solution)/shard_map/ppermute | solution.py:21
  208.9 10.3 %collective-permute-start.4 = (f32[300,1,130]{0,2,1:T(8,128)S(1)}, f32[300,1,130]{0,2,1:T(8,128)S(1)}, u32[]{:S(2)}, u32[]{:S(2)}) collective-permute-start(f32[300,1,130]{0,2,1:T(8,128)S(1)} %get-tuple-element.29), channel_id=1, source_target_pairs={{1,0},{2,1},{3,2},{4,3},{5,4},{6,5},{7,6},{8,7},{9,8},{10,9},{11,1... | collective-permute-start | bytes 468008 | tf_op jit(solution)/shard_map/ppermute | solution.py:21
  210.2 9.0 %copy-start.7 = (f32[300,8,128]{0,2,1:T(8,128)S(1)}, f32[300,8,128]{0,2,1:T(8,128)}, u32[]{:S(2)}) copy-start(f32[300,8,128]{0,2,1:T(8,128)} %copy.151) | copy-start | bytes 3686404
  210.2 9.0 %collective-permute-start.5 = (f32[300,1,130]{0,2,1:T(8,128)S(1)}, f32[300,1,130]{0,2,1:T(8,128)S(1)}, u32[]{:S(2)}, u32[]{:S(2)}) collective-permute-start(f32[300,1,130]{0,2,1:T(8,128)S(1)} %get-tuple-element.30), channel_id=1, source_target_pairs={{0,1},{1,2},{2,3},{3,4},{4,5},{5,6},{6,7},{7,8},{8,9},{9,10},{10,1... | collective-permute-start | bytes 468008 | tf_op jit(solution)/shard_map/ppermute | solution.py:18
  388.9 11.8 %collective-permute-start.6 = (f32[300,8,1]{0,1,2:T(8,128)S(1)}, f32[300,8,1]{0,1,2:T(8,128)S(1)}, u32[]{:S(2)}, u32[]{:S(2)}) collective-permute-start(f32[300,8,1]{0,1,2:T(8,128)S(1)} %copy.191), channel_id=1, source_target_pairs={{0,32},{32,64},{64,96},{96,128},{128,160},{160,192},{192,224},{1,3... | collective-permute-start | bytes 28808 | tf_op jit(solution)/shard_map/ppermute | solution.py:18
  393.4 7.3 %collective-permute-start.7 = (f32[300,8,1]{0,1,2:T(8,128)S(1)}, f32[300,8,1]{0,1,2:T(8,128)S(1)}, u32[]{:S(2)}, u32[]{:S(2)}) collective-permute-start(f32[300,8,1]{0,1,2:T(8,128)S(1)} %copy.192), channel_id=1, source_target_pairs={{32,0},{64,32},{96,64},{128,96},{160,128},{192,160},{224,192},{33,... | collective-permute-start | bytes 28808 | tf_op jit(solution)/shard_map/ppermute | solution.py:21
  401.8 10.7 %collective-permute-start.8 = (f32[300,1,130]{0,2,1:T(8,128)S(1)}, f32[300,1,130]{0,2,1:T(8,128)S(1)}, u32[]{:S(2)}, u32[]{:S(2)}) collective-permute-start(f32[300,1,130]{0,2,1:T(8,128)S(1)} %get-tuple-element.27), channel_id=1, source_target_pairs={{1,0},{2,1},{3,2},{4,3},{5,4},{6,5},{7,6},{8,7},{9,8},{10,9},{11,1... | collective-permute-start | bytes 468008 | tf_op jit(solution)/shard_map/ppermute | solution.py:21
  403.1 9.4 %copy-start.8 = (f32[300,8,128]{0,2,1:T(8,128)S(1)}, f32[300,8,128]{0,2,1:T(8,128)}, u32[]{:S(2)}) copy-start(f32[300,8,128]{0,2,1:T(8,128)} %copy.162) | copy-start | bytes 3686404
  403.1 9.4 %collective-permute-start.9 = (f32[300,1,130]{0,2,1:T(8,128)S(1)}, f32[300,1,130]{0,2,1:T(8,128)S(1)}, u32[]{:S(2)}, u32[]{:S(2)}) collective-permute-start(f32[300,1,130]{0,2,1:T(8,128)S(1)} %get-tuple-element.28), channel_id=1, source_target_pairs={{0,1},{1,2},{2,3},{3,4},{4,5},{5,6},{6,7},{7,8},{8,9},{9,10},{10,1... | collective-permute-start | bytes 468008 | tf_op jit(solution)/shard_map/ppermute | solution.py:18
  582.2 2.3 copy-start.1
  582.5 2.0 copy-start.2
  588.0 11.7 %copy-start.3 = (f32[38,8,8,128]{3,2,1,0:T(8,128)S(1)}, f32[38,8,8,128]{3,2,1,0:T(8,128)}, u32[]{:S(2)}) copy-start(f32[38,8,8,128]{3,2,1,0:T(8,128)} %copy-done.2) | copy-start | bytes 3735556
  588.0 15.8 %collective-permute-start.10 = (f32[300,8,1]{0,1,2:T(8,128)S(1)}, f32[300,8,1]{0,1,2:T(8,128)S(1)}, u32[]{:S(2)}, u32[]{:S(2)}) collective-permute-start(f32[300,8,1]{0,1,2:T(8,128)S(1)} %copy.193), channel_id=1, source_target_pairs={{0,32},{32,64},{64,96},{96,128},{128,160},{160,192},{192,224},{1,3... | collective-permute-start | bytes 28808 | tf_op jit(solution)/shard_map/ppermute | solution.py:18
  591.5 12.3 %collective-permute-start.11 = (f32[300,8,1]{0,1,2:T(8,128)S(1)}, f32[300,8,1]{0,1,2:T(8,128)S(1)}, u32[]{:S(2)}, u32[]{:S(2)}) collective-permute-start(f32[300,8,1]{0,1,2:T(8,128)S(1)} %copy.194), channel_id=1, source_target_pairs={{32,0},{64,32},{96,64},{128,96},{160,128},{192,160},{224,192},{33,... | collective-permute-start | bytes 28808 | tf_op jit(solution)/shard_map/ppermute | solution.py:21
  604.9 11.3 %collective-permute-start.12 = (f32[300,1,130]{0,2,1:T(8,128)S(1)}, f32[300,1,130]{0,2,1:T(8,128)S(1)}, u32[]{:S(2)}, u32[]{:S(2)}) collective-permute-start(f32[300,1,130]{0,2,1:T(8,128)S(1)} %get-tuple-element.25), channel_id=1, source_target_pairs={{1,0},{2,1},{3,2},{4,3},{5,4},{6,5},{7,6},{8,7},{9,8},{10,9},{11,1... | collective-permute-start | bytes 468008 | tf_op jit(solution)/shard_map/ppermute | solution.py:21
  606.2 10.0 %copy-start.6 = (f32[300,8,128]{0,2,1:T(8,128)S(1)}, f32[300,8,128]{0,2,1:T(8,128)}, u32[]{:S(2)}) copy-start(f32[300,8,128]{0,2,1:T(8,128)} %copy.173) | copy-start | bytes 3686404
  606.2 10.0 %collective-permute-start.13 = (f32[300,1,130]{0,2,1:T(8,128)S(1)}, f32[300,1,130]{0,2,1:T(8,128)S(1)}, u32[]{:S(2)}, u32[]{:S(2)}) collective-permute-start(f32[300,1,130]{0,2,1:T(8,128)S(1)} %get-tuple-element.26), channel_id=1, source_target_pairs={{0,1},{1,2},{2,3},{3,4},{4,5},{5,6},{6,7},{7,8},{8,9},{9,10},{10,1... | collective-permute-start | bytes 468008 | tf_op jit(solution)/shard_map/ppermute | solution.py:18
  (1 other events, 1.8 us)
